TPU v7x, 32 devices: a whole 2x2x4 slice. The times are simulated.
32 devices in a mesh: row: 8 (over z, y), col: 4 (over x, core).
Axes of the slice: x: 2, y: 2, z: 4, core: 2. Of those that a mesh axis runs over, the one named last changes fastest.
Arguments:
- upper: bfloat16 [4096, 8, 4, 128], P('row', None, 'col'), as said below
- signs: int32 [4096, 512], P(('row', 'col')), may hold values from 0 to 1
- weights: float32 [4096], P(('row', 'col')), may hold values from 0.5 to 2
- components: float32 [2], replicated, may hold values from 0.3 to 3
Outputs:
- applied: float32 [4096, 512], P(('row', 'col'))
Inputs may be any that keep to these rules, and one draw needn't show every extreme that they name: upper's first dimension and its flattened column index count the same samples in the same order.
All inputs are finite; a program needn't handle non-finite values.
Results may differ from a plain program's by a relative error of at most 0.0055.
Values may be sent and summed in bfloat16 or wider, within the bound.
No kernel may reach another device: no remote copies, remote signals or barrier semaphores. Data moves between devices by JAX's collectives and lax.ppermute only.
A program may use at most 128 MiB of HBM per device.

v0:
```python
import jax
import jax.numpy as jnp
from jax import lax
from jax.sharding import PartitionSpec as P


def body(upper, signs, weights, components):
    rows, ntiles, single, fine = upper.shape
    row_index = lax.axis_index("row")
    col_index = lax.axis_index("col")
    flat = upper.reshape(rows, ntiles * fine)
    probes = ((2 * signs - 1).astype(jnp.float32) * weights[:, None]).astype(jnp.bfloat16)
    q_rows = lax.all_gather(probes, "col", axis=0, tiled=True)
    zero = jnp.zeros((), jnp.bfloat16)
    rowpos = lax.broadcasted_iota(jnp.int32, (rows, ntiles, fine), 0)
    tilepos = lax.broadcasted_iota(jnp.int32, (rows, ntiles, fine), 1)
    colpos = col_index * fine + lax.broadcasted_iota(jnp.int32, (rows, ntiles, fine), 2)
    beyond = tilepos > row_index
    onside = tilepos == row_index
    keep_up = (beyond | onside & (colpos >= rowpos)).reshape(rows, ntiles * fine)
    keep_strict = (beyond | onside & (colpos > rowpos)).reshape(rows, ntiles * fine)
    masked_a = jnp.where(keep_up, flat, zero)
    masked_b = jnp.where(keep_strict, flat, zero)
    columns = masked_a
    direct = jnp.dot(
        columns,
        lax.all_gather(probes, "row", axis=0, tiled=True),
        preferred_element_type=jnp.float32,
    )
    columns = masked_b
    mirrored = lax.psum_scatter(
        lax.dot_general(
            columns, q_rows, (((0,), (0,)), ((), ())), preferred_element_type=jnp.float32
        ).astype(jnp.bfloat16),
        "row",
        scatter_dimension=0,
        tiled=True,
    ).astype(jnp.float32)
    summed = lax.psum_scatter(direct, "col", scatter_dimension=0, tiled=True)
    return components[0] * (summed + mirrored) + components[1] * probes.astype(jnp.float32)


def solution(mesh):
    return jax.shard_map(
        body,
        mesh=mesh,
        in_specs=(P("row", None, "col", None), P(("row", "col"), None), P(("row", "col")), P()),
        out_specs=P(("row", "col"), None),
        check_vma=False,
    )
```

profile of v0, /device:TPU:0, one launch (start us, length us, event | category | flops | bytes accessed | tf_op | source)
XLA Modules:
  0.0 154.1 jit_solution(2603484826157275666)
XLA Ops:
  6.5 0.0 copy-start.3
  6.5 0.0 all-gather.2.cloned.1.call-start
  6.5 1.8 %multiply_convert_fusion = bf16[128,512]{1,0:T(8,128)(2,1)} fusion(s32[128,512]{1,0:T(8,128)} %param.5, f32[128]{0:T(128)} %param.6), kind=kLoop, calls=%fused_computation.23 | loop fusion | flops 327680 | bytes 393728 | tf_op jit(solution)/shard_map/convert_element_type | solution.py:12
  8.3 0.0 all-gather.2.cloned.1.call-update
  8.3 0.0 reduce-scatter.5.cloned.1.call-start
  8.4 8.8 %all_gather.7 = bf16[512,512]{1,0:T(8,128)(2,1)S(1)} all-gather(bf16[128,512]{1,0:T(8,128)(2,1)} %multiply_convert_fusion), channel_id=1, replica_groups=mesh['row'=8,'col'=4] {'col'}, dimensions={0}, use_global_device_ids=true | all-gather | bytes 655360 | tf_op jit(solution)/shard_map/all_gather | solution.py:13
  17.3 0.1 broadcast_bitcast_fusion.1
  17.3 0.1 broadcast_bitcast_fusion.2
  17.4 0.0 copy-done.3
  17.4 1.8 %convolution_convert_fusion = bf16[1024,512]{1,0:T(8,128)(2,1)} fusion(bf16[512,512]{1,0:T(8,128)(2,1)S(1)} %all_gather.7, s32[1024]{0:T(1024)S(1)} %broadcast_bitcast_fusion, pred[1024]{0:T(1024)(128)(4,1)S(1)} %broadcast_bitcast_fusion.1, pred[1024]{0:T(1024)(128)(4,1)S(1)} %broadcast_bitcast_fusion.2, bf16[64,8,8,128]{3,2,1,0:T(8,128)(2,1)S(1)} %bitcast.22), kind=kOutput, calls=%fused_computation.8 | convolution fusion | flops 539492352 | bytes 2627584 | tf_op jit(solution)/shard_map/dot_general | solution.py:32
  19.2 0.0 reduce-scatter.5.cloned.1.call-update
  19.2 0.0 reduce-scatter.3.cloned.1.call-start
  19.3 33.1 %all-gather.2.cloned.1.call-done = bf16[1024,512]{1,0:T(8,128)(2,1)} async-done(((bf16[128,512]{1,0:T(8,128)(2,1)}), bf16[1024,512]{1,0:T(8,128)(2,1)}) %all-gather.2.cloned.1.call-update) | async-done | bytes 1048592 | tf_op jit(solution)/shard_map/all_gather | solution.py:27
  52.4 3.0 %fusion.7 = f32[512,512]{1,0:T(8,128)} fusion(bf16[1024,512]{1,0:T(8,128)(2,1)} %all-gather.2.cloned.1.call-done, s32[1024]{0:T(1024)S(1)} %broadcast_bitcast_fusion, pred[1024]{0:T(1024)(128)(4,1)S(1)} %broadcast_bitcast_fusion.1, pred[1024]{0:T(1024)(128)(4,1)S(1)} %broadcast_bitcast_fusion.2, bf16[64,8,8,128]{3,2,1,0:T(8,128)(2,1)S(1)} %bitcast.23), kind=kOutput, calls=%fused_computation.9 | convolution fusion | flops 538968064 | bytes 3151872 | tf_op jit(solution)/shard_map/dot_general | solution.py:25
  55.3 0.0 copy-start.2
  55.3 0.0 copy-start
  55.3 0.0 copy-start.1
  55.3 0.0 reduce-scatter.3.cloned.1.call-update
  55.4 0.6 copy-done.2
  56.0 0.6 fusion.23
  56.6 61.3 %reduce-scatter.5.cloned.1.call-done = bf16[128,512]{1,0:T(8,128)(2,1)} async-done(((bf16[1024,512]{1,0:T(8,128)(2,1)}), bf16[128,512]{1,0:T(8,128)(2,1)}) %reduce-scatter.5.cloned.1.call-update) | async-done | bytes 131088 | tf_op jit(solution)/shard_map/reduce_scatter | solution.py:31
  117.9 26.6 %reduce-scatter.3.cloned.1.call-done = f32[128,512]{1,0:T(8,128)} async-done(((f32[512,512]{1,0:T(8,128)}), f32[128,512]{1,0:T(8,128)}) %reduce-scatter.3.cloned.1.call-update) | async-done | bytes 262160 | tf_op jit(solution)/shard_map/reduce_scatter | solution.py:39
  144.5 0.0 copy-done
  144.5 0.0 copy-done.1
  144.5 3.1 %multiply_add_fusion = f32[128,512]{1,0:T(8,128)} fusion(f32[128,512]{1,0:T(8,128)} %reduce-scatter.3.cloned.1.call-done, bf16[128,512]{1,0:T(8,128)(2,1)} %reduce-scatter.5.cloned.1.call-done, f32[]{:T(128)} %bitcast.4, f32[]{:T(128)} %bitcast, f32[128]{0:T(128)S(1)} %copy-done.1, s32[128,512]{1,0:T(8,128)S(1)} %copy-done), kind=kLoop, calls=%fused_computation.22 | loop fusion | flops 720896 | bytes 918024 | tf_op jit(solution)/shard_map/add | solution.py:40
  (3 shorter events, 0.0 us)
Async XLA Ops:
  6.5 10.9 %copy-start.3 = (bf16[512,8,1,128]{3,1,2,0:T(8,128)(2,1)S(1)}, bf16[512,8,1,128]{3,1,2,0:T(8,128)(2,1)}, u32[]{:S(2)}) copy-start(bf16[512,8,1,128]{3,1,2,0:T(8,128)(2,1)} %param.4) | copy-start | bytes 3145732
  6.5 45.8 %all-gather.2.cloned.1.call-start = ((), (), s32[]{:S(2)}) async-start(), calls=%async_computation.2 | async-start | bytes 1179648 | tf_op jit(solution)/shard_map/all_gather | solution.py:27
  8.3 109.5 %reduce-scatter.5.cloned.1.call-start = ((), (), s32[]{:S(2)}) async-start(), calls=%async_computation.4 | async-start | bytes 1179648 | tf_op jit(solution)/shard_map/reduce_scatter | solution.py:31
  19.2 125.3 %reduce-scatter.3.cloned.1.call-start = ((), (), s32[]{:S(2)}) async-start(), calls=%async_computation.3 | async-start | bytes 1310720 | tf_op jit(solution)/shard_map/reduce_scatter | solution.py:39
  55.3 0.7 copy-start.2
  55.3 89.2 %copy-start = (s32[128,512]{1,0:T(8,128)S(1)}, s32[128,512]{1,0:T(8,128)}, u32[]{:S(2)}) copy-start(s32[128,512]{1,0:T(8,128)} %param.5) | copy-start | bytes 786436
  55.3 89.2 %copy-start.1 = (f32[128]{0:T(128)S(1)}, f32[128]{0:T(128)}, u32[]{:S(2)}) copy-start(f32[128]{0:T(128)} %param.6) | copy-start | bytes 1540
Sparse Core Ops, SparseCore 0:
  9.5 42.8 all-gather.1
  55.8 62.0 reduce-scatter.4
  120.6 23.8 reduce-scatter.2
where the time goes:
time: 154 us
  waiting for transfers between devices  121 us (79%)
  between operations  13.1 us (9%)
  blocking collectives  8.83 us (6%)
  other arithmetic  4.85 us (3%)
  matrix products  4.75 us (3%)
    reduce_scatter x1, waiting for transfers between devices, body(): lax.psum_scatter(lax.dot_general(columns, q_rows, (((0,), (0,)), ((), ())...  61.3 us
    all_gather x1, waiting for transfers between devices, body(): lax.all_gather(probes, 'row', axis=0, tiled=True)  33.1 us
    reduce_scatter x1, waiting for transfers between devices, body(): summed = lax.psum_scatter(direct, 'col', scatter_dimension=0, tiled=True)  26.6 us
    all_gather x1, blocking collectives, body(): q_rows = lax.all_gather(probes, 'col', axis=0, tiled=True)  8.83 us
  transfers between devices with their start and end apart: 3, of which 3 were waited for; matrix products, arithmetic and copies ran while one was open for 4% of the time, Pallas kernels for 0%

commit v1 on v0

--- a/solution.py
+++ b/solution.py
@@ -2,6 +2,18 @@
 import jax.numpy as jnp
 from jax import lax
 from jax.sharding import PartitionSpec as P
+
+
+def doubled_up(x, axis, dim):
+    ways, here, lap = (lax.axis_size(axis), lax.axis_index(axis), x.shape[dim])
+    line, have = (x, 1)
+    while have < ways:
+        line = jnp.concatenate(
+            [line, lax.ppermute(line, axis, [(d, (d - have) % ways) for d in range(ways)])],
+            axis=dim,
+        )
+        have = 2 * have
+    return jnp.roll(line, here * lap, axis=dim)
 
 
 def body(upper, signs, weights, components):
@@ -22,11 +34,7 @@
     masked_a = jnp.where(keep_up, flat, zero)
     masked_b = jnp.where(keep_strict, flat, zero)
     columns = masked_a
-    direct = jnp.dot(
-        columns,
-        lax.all_gather(probes, "row", axis=0, tiled=True),
-        preferred_element_type=jnp.float32,
-    )
+    direct = jnp.dot(columns, doubled_up(probes, "row", 0), preferred_element_type=jnp.float32)
     columns = masked_b
     mirrored = lax.psum_scatter(
         lax.dot_general(

time: 154 us -> 137 us (0.89)
  waiting for transfers between devices: 121 us -> 91.7 us
  starting transfers between devices: 0.09 us -> 6.3 us
  local copies, waits for them, and re-layouts: 1.39 us -> 5.94 us
    ppermute x0 -> x3, waiting for transfers between devices: none -> 40.4 us  [doubled_up(): lax.ppermute(line, axis, [(d, (d - have) % ways) for d in range(ways)])]
    reduce_scatter x1, waiting for transfers between devices: 61.3 us -> 24.6 us  [body(): lax.psum_scatter(lax.dot_general(columns, q_rows, (((0,), (0,)), ((), ())...]
    all_gather x1 -> x0, waiting for transfers between devices: 33.1 us -> none  [body(): lax.all_gather(probes, 'row', axis=0, tiled=True)]
    ppermute x0 -> x3, starting transfers between devices: none -> 6.26 us  [doubled_up(): lax.ppermute(line, axis, [(d, (d - have) % ways) for d in range(ways)])]
    unnamed x8 -> x10, local copies, waits for them, and re-layouts: 0.64 us -> 4.29 us
    convert_element_type x1 -> x0, other arithmetic: 1.78 us -> none  [body(): ((2 * signs - 1).astype(jnp.float32) * weights[:, None]).astype(jnp.bfloa...]
    unnamed x0 -> x1, other arithmetic: none -> 1.71 us
  transfers between devices with their start and end apart: 3 -> 5, of which waited for: 3 -> 5; matrix products, arithmetic and copies ran while one was open for 4% -> 6% of each run, Pallas kernels for 0% -> 0%
where the time goes in v1:
time: 137 us
  waiting for transfers between devices  91.7 us (67%)
  between operations  13.5 us (10%)
  blocking collectives  8.6 us (6%)
  starting transfers between devices  6.3 us (5%)
  matrix products  5.98 us (4%)
  local copies, waits for them, and re-layouts  5.94 us (4%)
  other arithmetic  4.82 us (4%)
    ppermute x3, waiting for transfers between devices, doubled_up(): lax.ppermute(line, axis, [(d, (d - have) % ways) for d in range(ways)])  40.4 us
    reduce_scatter x1, waiting for transfers between devices, body(): summed = lax.psum_scatter(direct, 'col', scatter_dimension=0, tiled=True)  26.6 us
    reduce_scatter x1, waiting for transfers between devices, body(): lax.psum_scatter(lax.dot_general(columns, q_rows, (((0,), (0,)), ((), ())...  24.6 us
    all_gather x1, blocking collectives, body(): q_rows = lax.all_gather(probes, 'col', axis=0, tiled=True)  8.6 us
    ppermute x3, starting transfers between devices, doubled_up(): lax.ppermute(line, axis, [(d, (d - have) % ways) for d in range(ways)])  6.26 us
    unnamed x10, local copies, waits for them, and re-layouts  4.29 us
    add x1, other arithmetic, body(): components[0] * (summed + mirrored)  3.05 us
    dot_general x1, matrix products, body(): lax.dot_general(columns, q_rows, (((0,), (0,)), ((), ())), preferred_elem...  3.03 us
  transfers between devices with their start and end apart: 5, of which 5 were waited for; matrix products, arithmetic and copies ran while one was open for 6% of the time, Pallas kernels for 0%

profile of v1, /device:TPU:0, one launch (start us, length us, event | category | flops | bytes accessed | tf_op | source)
XLA Modules:
  0.0 136.8 jit_solution(1946478852003145615)
XLA Ops:
  6.5 0.0 reduce-scatter.5.cloned.1.call-start
  6.5 0.1 broadcast_bitcast_fusion.1
  6.6 0.1 broadcast_bitcast_fusion.2
  6.7 1.7 %constant_dynamic-update-slice_fusion.7 = (bf16[2048,512]{1,0:T(8,128)(2,1)}, bf16[128,512]{1,0:T(8,128)(2,1)S(1)}) fusion(f32[128]{0:T(128)} %param.6, s32[128,512]{1,0:T(8,128)} %param.5), kind=kLoop, calls=%fused_computation.34 | loop fusion | flops 327679 | bytes 524800
  8.4 8.6 %all_gather.3 = bf16[512,512]{1,0:T(8,128)(2,1)S(1)} all-gather(bf16[128,512]{1,0:T(8,128)(2,1)S(1)} %get-tuple-element.6), channel_id=1, replica_groups=mesh['row'=8,'col'=4] {'col'}, dimensions={0}, use_global_device_ids=true | all-gather | bytes 655360 | tf_op jit(solution)/shard_map/all_gather | solution.py:25
  17.0 3.0 %convolution_convert_fusion = bf16[1024,512]{1,0:T(8,128)(2,1)} fusion(bf16[512,512]{1,0:T(8,128)(2,1)S(1)} %all_gather.3, s32[1024]{0:T(1024)S(1)} %broadcast_bitcast_fusion, pred[1024]{0:T(1024)(128)(4,1)S(1)} %broadcast_bitcast_fusion.1, pred[1024]{0:T(1024)(128)(4,1)S(1)} %broadcast_bitcast_fusion.2, bf16[64,8,8,128]{3,2,1,0:T(8,128)(2,1)} %bitcast.21), kind=kOutput, calls=%fused_computation.8 | convolution fusion | flops 539492352 | bytes 2627584 | tf_op jit(solution)/shard_map/dot_general | solution.py:40
  20.0 0.0 reduce-scatter.5.cloned.1.call-update
  20.1 0.0 reduce-scatter.3.cloned.1.call-start
  20.1 4.6 %collective-permute-start = (bf16[128,512]{1,0:T(8,128)(2,1)S(1)}, bf16[128,512]{1,0:T(8,128)(2,1)S(1)}, u32[]{:S(2)}, u32[]{:S(2)}) collective-permute-start(bf16[128,512]{1,0:T(8,128)(2,1)S(1)} %get-tuple-element.6), channel_id=1, source_target_pairs={{0,28},{4,0},{8,4},{12,8},{16,12},{20,16},{24,20},{28,24},{1,29},{... | collective-permute-start | bytes 393224 | tf_op jit(solution)/shard_map/ppermute | solution.py:12
  24.7 3.3 %collective-permute-done = bf16[128,512]{1,0:T(8,128)(2,1)S(1)} collective-permute-done((bf16[128,512]{1,0:T(8,128)(2,1)S(1)}, bf16[128,512]{1,0:T(8,128)(2,1)S(1)}, u32[]{:S(2)}, u32[]{:S(2)}) %collective-permute-start) | collective-permute-done | bytes 131104 | tf_op jit(solution)/shard_map/ppermute | solution.py:12
  28.0 1.6 %collective-permute-start.1 = (bf16[256,512]{1,0:T(8,128)(2,1)S(1)}, bf16[256,512]{1,0:T(8,128)(2,1)S(1)}, u32[]{:S(2)}, u32[]{:S(2)}) collective-permute-start(bf16[256,512]{1,0:T(8,128)(2,1)S(1)} %pad_maximum_fusion.1), channel_id=1, source_target_pairs={{0,24},{4,28},{8,0},{12,4},{16,8},{20,12},{24,16},{28,20},{1,25},{... | collective-permute-start | bytes 786440 | tf_op jit(solution)/shard_map/ppermute | solution.py:12
  29.6 9.8 %collective-permute-done.1 = bf16[256,512]{1,0:T(8,128)(2,1)S(1)} collective-permute-done((bf16[256,512]{1,0:T(8,128)(2,1)S(1)}, bf16[256,512]{1,0:T(8,128)(2,1)S(1)}, u32[]{:S(2)}, u32[]{:S(2)}) %collective-permute-start.1) | collective-permute-done | bytes 262176 | tf_op jit(solution)/shard_map/ppermute | solution.py:12
  39.5 0.0 copy-start.1
  39.5 0.1 collective-permute-start.2
  39.6 0.7 constant_dynamic-update-slice_fusion.6
  40.3 0.7 constant_dynamic-update-slice_fusion.5
  41.0 27.3 %collective-permute-done.2 = bf16[512,512]{1,0:T(8,128)(2,1)S(1)} collective-permute-done((bf16[512,512]{1,0:T(8,128)(2,1)S(1)}, bf16[512,512]{1,0:T(8,128)(2,1)S(1)}, u32[]{:S(2)}, u32[]{:S(2)}) %collective-permute-start.2) | collective-permute-done | bytes 524320 | tf_op jit(solution)/shard_map/ppermute | solution.py:12
  68.2 0.8 constant_dynamic-update-slice_fusion.4
  69.1 0.7 constant_dynamic-update-slice_fusion.3
  69.7 0.7 constant_dynamic-update-slice_fusion.2
  70.4 0.7 constant_dynamic-update-slice_fusion.1
  71.1 0.8 constant_dynamic-update-slice_fusion
  72.0 0.0 copy-done.1
  72.0 0.0 copy-start
  72.0 3.0 %fusion.7 = f32[512,512]{1,0:T(8,128)} fusion(bf16[2048,512]{1,0:T(8,128)(2,1)} %constant_dynamic-update-slice_fusion, s32[]{:T(128)S(6)} %select_n.22, s32[1024]{0:T(1024)S(1)} %broadcast_bitcast_fusion, pred[1024]{0:T(1024)(128)(4,1)S(1)} %broadcast_bitcast_fusion.1, pred[1024]{0:T(1024)(128)(4,1)S(1)} %broadcast_bitcast_fusion.2, ...), kind=kOutput, calls=%fused_computation.9 | convolution fusion | flops 538968064 | bytes 3151876 | tf_op jit(solution)/shard_map/dot_general | solution.py:37
  74.9 0.0 reduce-scatter.3.cloned.1.call-update
  74.9 0.0 copy-done
  75.0 0.7 fusion.25
  75.6 24.6 %reduce-scatter.5.cloned.1.call-done = bf16[128,512]{1,0:T(8,128)(2,1)} async-done(((bf16[1024,512]{1,0:T(8,128)(2,1)}), bf16[128,512]{1,0:T(8,128)(2,1)}) %reduce-scatter.5.cloned.1.call-update) | async-done | bytes 131088 | tf_op jit(solution)/shard_map/reduce_scatter | solution.py:39
  100.2 26.6 %reduce-scatter.3.cloned.1.call-done = f32[128,512]{1,0:T(8,128)} async-done(((f32[512,512]{1,0:T(8,128)}), f32[128,512]{1,0:T(8,128)}) %reduce-scatter.3.cloned.1.call-update) | async-done | bytes 262160 | tf_op jit(solution)/shard_map/reduce_scatter | solution.py:47
  126.9 3.1 %multiply_add_fusion = f32[128,512]{1,0:T(8,128)} fusion(bf16[128,512]{1,0:T(8,128)(2,1)S(1)} %get-tuple-element.6, f32[128,512]{1,0:T(8,128)} %reduce-scatter.3.cloned.1.call-done, bf16[128,512]{1,0:T(8,128)(2,1)} %reduce-scatter.5.cloned.1.call-done, f32[]{:T(128)} %bitcast.4, f32[]{:T(128)} %bitcast), kind=kLoop, calls=%fused_computation.25 | loop fusion | flops 393216 | bytes 786440 | tf_op jit(solution)/shard_map/add | solution.py:48
  (5 shorter events, 0.1 us)
Async XLA Ops:
  6.5 93.7 %reduce-scatter.5.cloned.1.call-start = ((), (), s32[]{:S(2)}) async-start(), calls=%async_computation.3 | async-start | bytes 1179648 | tf_op jit(solution)/shard_map/reduce_scatter | solution.py:39
  20.1 106.8 %reduce-scatter.3.cloned.1.call-start = ((), (), s32[]{:S(2)}) async-start(), calls=%async_computation.2 | async-start | bytes 1310720 | tf_op jit(solution)/shard_map/reduce_scatter | solution.py:47
  20.1 7.9 %collective-permute-start = (bf16[128,512]{1,0:T(8,128)(2,1)S(1)}, bf16[128,512]{1,0:T(8,128)(2,1)S(1)}, u32[]{:S(2)}, u32[]{:S(2)}) collective-permute-start(bf16[128,512]{1,0:T(8,128)(2,1)S(1)} %get-tuple-element.6), channel_id=1, source_target_pairs={{0,28},{4,0},{8,4},{12,8},{16,12},{20,16},{24,20},{28,24},{1,29},{... | collective-permute-start | bytes 393224 | tf_op jit(solution)/shard_map/ppermute | solution.py:12
  28.0 11.4 %collective-permute-start.1 = (bf16[256,512]{1,0:T(8,128)(2,1)S(1)}, bf16[256,512]{1,0:T(8,128)(2,1)S(1)}, u32[]{:S(2)}, u32[]{:S(2)}) collective-permute-start(bf16[256,512]{1,0:T(8,128)(2,1)S(1)} %pad_maximum_fusion.1), channel_id=1, source_target_pairs={{0,24},{4,28},{8,0},{12,4},{16,8},{20,12},{24,16},{28,20},{1,25},{... | collective-permute-start | bytes 786440 | tf_op jit(solution)/shard_map/ppermute | solution.py:12
  39.5 32.5 %copy-start.1 = (bf16[512,8,1,128]{3,1,2,0:T(8,128)(2,1)S(1)}, bf16[512,8,1,128]{3,1,2,0:T(8,128)(2,1)}, u32[]{:S(2)}) copy-start(bf16[512,8,1,128]{3,1,2,0:T(8,128)(2,1)} %param.4) | copy-start | bytes 3145732
  39.5 28.8 %collective-permute-start.2 = (bf16[512,512]{1,0:T(8,128)(2,1)S(1)}, bf16[512,512]{1,0:T(8,128)(2,1)S(1)}, u32[]{:S(2)}, u32[]{:S(2)}) collective-permute-start(bf16[512,512]{1,0:T(8,128)(2,1)S(1)} %pad_maximum_fusion), channel_id=1, source_target_pairs={{0,16},{4,20},{8,24},{12,28},{16,0},{20,4},{24,8},{28,12},{1,17},{... | collective-permute-start | bytes 1572872 | tf_op jit(solution)/shard_map/ppermute | solution.py:12
  72.0 3.0 %copy-start = (f32[2]{0:T(128)S(1)}, f32[2]{0:T(128)}, u32[]{:S(2)}) copy-start(f32[2]{0:T(128)} %param.7) | copy-start | bytes 28
Sparse Core Ops, SparseCore 0:
  20.2 79.9 reduce-scatter.4
  102.9 23.9 reduce-scatter.2
